TPU v7x, 256 devices: a whole 4x4x8 slice. The times are simulated.
256 devices in a mesh: pipe: 8 (over z_lo, core), seq: 32 (over z_hi, y, x).
Axes of the slice: x: 4, y: 4, z: 8 (z_hi: 2, z_lo: 4; z = z_hi * 4 + z_lo), core: 2. Of those that a mesh axis runs over, the one named last changes fastest.
Arguments:
- queries: bfloat16 [8, 4096, 12288], P('pipe', 'seq'), may hold values from -6 to 6
- keys: bfloat16 [8, 4096, 12288], P('pipe', 'seq'), may hold values from -6 to 6
- values: bfloat16 [8, 4096, 8192], P('pipe', 'seq'), may hold values from -6 to 6
- doc_lengths: int32 [8, 16], replicated, may hold values from 1 to 512, 4096 in all within a row
Outputs:
- mtp_attention: bfloat16 [8, 4096, 8192], P('pipe', 'seq')
All inputs are finite; a program needn't handle non-finite values.
Results may differ from a plain program's by a relative error of at most 0.0046.
Values may be sent and summed in bfloat16 or wider, within the bound.
No kernel may reach another device: no remote copies, remote signals or barrier semaphores. Data moves between devices by JAX's collectives and lax.ppermute only.
A program may use at most 128 MiB of HBM per device.

v0:
```python
import jax
import jax.numpy as jnp
from jax import lax
from jax.sharding import PartitionSpec as P

HEADS = 64
DQK = 192
DV = 128


def shifted(block, axis, distance):
    devices = range(lax.axis_size(axis))
    route = [((i - distance) % len(devices), i) for i in devices]
    return lax.ppermute(block, axis, route)


def attend(queries, keys, values, lengths_here):
    seq_count = lax.axis_size("seq")
    local_rows = queries.shape[1]
    per_device = HEADS // seq_count
    query_split = queries.reshape(local_rows, seq_count, per_device * DQK)
    key_split = keys.reshape(local_rows, seq_count, per_device * DQK)
    value_split = values.reshape(local_rows, seq_count, per_device * DV)
    query_all, key_all, value_all = (
        lax.all_to_all(query_split, "seq", split_axis=1, concat_axis=0, tiled=True),
        lax.all_to_all(key_split, "seq", split_axis=1, concat_axis=0, tiled=True),
        lax.all_to_all(value_split, "seq", split_axis=1, concat_axis=0, tiled=True),
    )
    all_rows = local_rows * seq_count
    query_all = query_all.reshape(all_rows, per_device, DQK)
    key_all = key_all.reshape(all_rows, per_device, DQK)
    value_all = value_all.reshape(all_rows, per_device, DV)
    position = jnp.arange(all_rows, dtype=jnp.int32)
    doc_ends = jnp.cumsum(lengths_here)
    document = jnp.sum((doc_ends[None, :] <= position[:, None]).astype(jnp.int32), axis=1)
    block_rows = all_rows // 8
    score_scale = DQK ** (-0.5)
    pieces = []
    for number in range(8):
        row_start = number * block_rows
        row_stop = row_start + block_rows
        first_column = max(0, number - 1)
        key_start = first_column * block_rows
        query_block = query_all[row_start:row_stop]
        visible = (document[row_start:row_stop, None] == document[None, key_start:row_stop]) & (
            position[None, key_start:row_stop] <= position[row_start:row_stop, None]
        )
        scores = jnp.einsum(
            "qhd,khd->hqk",
            query_block,
            key_all[key_start:row_stop],
            preferred_element_type=jnp.float32,
        )
        scores = jnp.where(visible[None], scores * score_scale, -jnp.inf)
        row_max = jnp.max(scores, axis=2, keepdims=True)
        exponent = jnp.exp(scores - row_max)
        weights = (exponent / jnp.sum(exponent, axis=2, keepdims=True)).astype(jnp.bfloat16)
        mixed_out = jnp.einsum(
            "hqk,khd->qhd",
            weights,
            value_all[key_start:row_stop],
            preferred_element_type=jnp.float32,
        )
        pieces.append(mixed_out.astype(jnp.bfloat16).reshape(block_rows, per_device * DV))
    attended = jnp.concatenate(pieces, axis=0).reshape(seq_count, local_rows, per_device * DV)
    return lax.all_to_all(attended, "seq", split_axis=0, concat_axis=2, tiled=True)


def local(queries, keys, values, doc_lengths):
    segments = lax.axis_size("pipe")
    segment = lax.axis_index("pipe")
    moved = shifted((queries, keys, values), "pipe", 1)
    source = (segment + segments - 1) % segments
    lengths_here = lax.dynamic_index_in_dim(doc_lengths, source, 0, keepdims=False)
    return attend(moved[0], moved[1], moved[2], lengths_here)


def solution(mesh):
    placed = (P("pipe", "seq", None), P("pipe", "seq", None), P("pipe", "seq", None), P())
    return jax.shard_map(
        local, mesh=mesh, in_specs=placed, out_specs=P("pipe", "seq", None), check_vma=False
    )
```

profile of v0, /device:TPU:32, one launch (start us, length us, event | category | flops | bytes accessed | tf_op | source)
XLA Modules:
  0.0 479.2 jit_solution(719580533046521933)
XLA Ops:
  0.0 25.7 %collective-permute-done.2 = bf16[1,128,8192]{2,1,0:T(8,128)(2,1)S(1)} collective-permute-done((bf16[1,128,8192]{2,1,0:T(8,128)(2,1)}, bf16[1,128,8192]{2,1,0:T(8,128)(2,1)S(1)}, u32[]{:S(2)}, u32[]{:S(2)}) %collective-permute-start.2) | collective-permute-done | bytes 2097184 | tf_op jit(solution)/shard_map/ppermute | solution.py:14
  28.1 13.1 %all-to-all-start.2 = ((bf16[128,32,256]{0,2,1:T(8,128)(2,1)}), bf16[128,32,256]{0,2,1:T(8,128)(2,1)S(1)}, u32[]{:S(2)}, u32[]{:S(2)}) async-start(bf16[128,32,256]{0,2,1:T(8,128)(2,1)} %bitcast.164), calls=%async_computation.2 | async-start | bytes 4194304 | tf_op jit(solution)/shard_map/all_to_all | solution.py:27
  41.2 79.1 %collective-permute-done.1 = bf16[1,128,12288]{2,1,0:T(8,128)(2,1)} collective-permute-done((bf16[1,128,12288]{2,1,0:T(8,128)(2,1)}, bf16[1,128,12288]{2,1,0:T(8,128)(2,1)}, u32[]{:S(2)}, u32[]{:S(2)}) %collective-permute-start.1) | collective-permute-done | bytes 3145760 | tf_op jit(solution)/shard_map/ppermute | solution.py:14
  120.3 4.6 copy.82
  126.3 11.1 %all-to-all-start.1 = ((bf16[128,32,384]{0,2,1:T(8,128)(2,1)}), bf16[128,32,384]{0,2,1:T(8,128)(2,1)S(1)}, u32[]{:S(2)}, u32[]{:S(2)}) async-start(bf16[128,32,384]{0,2,1:T(8,128)(2,1)} %bitcast.163), calls=%async_computation.1 | async-start | bytes 6291456 | tf_op jit(solution)/shard_map/all_to_all | solution.py:26
  137.5 101.6 %collective-permute-done = bf16[1,128,12288]{2,1,0:T(8,128)(2,1)} collective-permute-done((bf16[1,128,12288]{2,1,0:T(8,128)(2,1)}, bf16[1,128,12288]{2,1,0:T(8,128)(2,1)}, u32[]{:S(2)}, u32[]{:S(2)}) %collective-permute-start) | collective-permute-done | bytes 3145760 | tf_op jit(solution)/shard_map/ppermute | solution.py:14
  239.1 4.7 copy.80
  243.8 12.0 %all-to-all-start = ((bf16[128,32,384]{0,2,1:T(8,128)(2,1)}), bf16[128,32,384]{0,2,1:T(8,128)(2,1)}, u32[]{:S(2)}, u32[]{:S(2)}) async-start(bf16[128,32,384]{0,2,1:T(8,128)(2,1)} %bitcast.162), calls=%async_computation | async-start | bytes 6291456 | tf_op jit(solution)/shard_map/all_to_all | solution.py:25
  266.6 3.8 fusion.88
  302.3 27.7 %all-to-all-done = bf16[128,32,384]{0,2,1:T(8,128)(2,1)} async-done(((bf16[128,32,384]{0,2,1:T(8,128)(2,1)}), bf16[128,32,384]{0,2,1:T(8,128)(2,1)}, u32[]{:S(2)}, u32[]{:S(2)}) %all-to-all-start) | async-done | bytes 3145760 | tf_op jit(solution)/shard_map/all_to_all | solution.py:25
  361.3 4.7 fusion.92
  366.0 3.3 fusion.50
  370.0 4.7 fusion.93
  374.8 3.2 fusion.49
  378.7 4.8 %fusion.94 = (f32[2,512]{1,0:T(2,128)S(1)}, f32[2,512,1024]{2,1,0:T(8,128)}) fusion(pred[512,1024]{1,0:T(8,128)(4,1)S(1)} %copy-done.20, bf16[512,2,192]{0,2,1:T(8,128)(2,1)} %slice.269, bf16[1024,2,192]{0,2,1:T(8,128)(2,1)S(1)} %copy-done.13), kind=kOutput, calls=%fused_computation.145 | convolution fusion | flops 406848512 | bytes 5902336 | tf_op jit(solution)/shard_map/sub | solution.py:56
  383.5 3.2 fusion.48
  387.5 4.8 %fusion.95 = (f32[2,512]{1,0:T(2,128)S(1)}, f32[2,512,1024]{2,1,0:T(8,128)}) fusion(pred[512,1024]{1,0:T(8,128)(4,1)S(1)} %copy-done.19, bf16[512,2,192]{0,2,1:T(8,128)(2,1)} %slice.279, bf16[1024,2,192]{0,2,1:T(8,128)(2,1)S(1)} %copy-done.12), kind=kOutput, calls=%fused_computation.146 | convolution fusion | flops 406848512 | bytes 5902336 | tf_op jit(solution)/shard_map/sub | solution.py:56
  392.3 3.2 fusion.47
  396.3 4.7 fusion.96
  404.9 4.7 fusion.97
  413.6 3.7 fusion.98
  421.1 3.3 copy.108
  424.4 48.4 %all_to_all.63 = bf16[32,128,256]{2,1,0:T(8,128)(2,1)} all-to-all(bf16[32,128,256]{2,1,0:T(8,128)(2,1)S(1)} %bitcast.165), channel_id=1, replica_groups=mesh['pipe'=8,'seq'=32] {'seq'}, dimensions={0} | all-to-all | bytes 4194304 | tf_op jit(solution)/shard_map/all_to_all | solution.py:66
  472.8 3.2 copy.109
  (161 shorter events, 95.1 us)
Async XLA Ops:
  0.0 255.9 %copy-start = (s32[8,16]{1,0:T(8,128)S(1)}, s32[8,16]{1,0:T(8,128)}, u32[]{:S(2)}) copy-start(s32[8,16]{1,0:T(8,128)} %param.7) | copy-start | bytes 1540
  0.0 25.7 %collective-permute-start.2 = (bf16[1,128,8192]{2,1,0:T(8,128)(2,1)}, bf16[1,128,8192]{2,1,0:T(8,128)(2,1)S(1)}, u32[]{:S(2)}, u32[]{:S(2)}) collective-permute-start(bf16[1,128,8192]{2,1,0:T(8,128)(2,1)} %param.6), channel_id=1, source_target_pairs={{224,0},{0,32},{32,64},{64,96},{96,128},{128,160},{160,192},{192,2... | collective-permute-start | bytes 6291464 | tf_op jit(solution)/shard_map/ppermute | solution.py:14
  28.1 96.9 %all-to-all-start.2 = ((bf16[128,32,256]{0,2,1:T(8,128)(2,1)}), bf16[128,32,256]{0,2,1:T(8,128)(2,1)S(1)}, u32[]{:S(2)}, u32[]{:S(2)}) async-start(bf16[128,32,256]{0,2,1:T(8,128)(2,1)} %bitcast.164), calls=%async_computation.2 | async-start | bytes 4194304 | tf_op jit(solution)/shard_map/all_to_all | solution.py:27
  41.2 79.2 %collective-permute-start.1 = (bf16[1,128,12288]{2,1,0:T(8,128)(2,1)}, bf16[1,128,12288]{2,1,0:T(8,128)(2,1)}, u32[]{:S(2)}, u32[]{:S(2)}) collective-permute-start(bf16[1,128,12288]{2,1,0:T(8,128)(2,1)} %param.5), channel_id=1, source_target_pairs={{224,0},{0,32},{32,64},{64,96},{96,128},{128,160},{160,192},{192,2... | collective-permute-start | bytes 9437192 | tf_op jit(solution)/shard_map/ppermute | solution.py:14
  126.3 117.5 %all-to-all-start.1 = ((bf16[128,32,384]{0,2,1:T(8,128)(2,1)}), bf16[128,32,384]{0,2,1:T(8,128)(2,1)S(1)}, u32[]{:S(2)}, u32[]{:S(2)}) async-start(bf16[128,32,384]{0,2,1:T(8,128)(2,1)} %bitcast.163), calls=%async_computation.1 | async-start | bytes 6291456 | tf_op jit(solution)/shard_map/all_to_all | solution.py:26
  137.4 101.7 %collective-permute-start = (bf16[1,128,12288]{2,1,0:T(8,128)(2,1)}, bf16[1,128,12288]{2,1,0:T(8,128)(2,1)}, u32[]{:S(2)}, u32[]{:S(2)}) collective-permute-start(bf16[1,128,12288]{2,1,0:T(8,128)(2,1)} %param.4), channel_id=1, source_target_pairs={{224,0},{0,32},{32,64},{64,96},{96,128},{128,160},{160,192},{192,2... | collective-permute-start | bytes 9437192 | tf_op jit(solution)/shard_map/ppermute | solution.py:14
  243.8 86.2 %all-to-all-start = ((bf16[128,32,384]{0,2,1:T(8,128)(2,1)}), bf16[128,32,384]{0,2,1:T(8,128)(2,1)}, u32[]{:S(2)}, u32[]{:S(2)}) async-start(bf16[128,32,384]{0,2,1:T(8,128)(2,1)} %bitcast.162), calls=%async_computation | async-start | bytes 6291456 | tf_op jit(solution)/shard_map/all_to_all | solution.py:25
  336.3 4.0 copy-start.9
  340.3 4.0 copy-start.8
  344.2 4.0 copy-start.7
  348.2 4.1 copy-start.6
  366.0 4.0 copy-start.14
  366.0 4.0 copy-start.22
  370.0 4.7 copy-start.27
  374.8 4.0 copy-start.20
  378.7 4.8 %copy-start.26 = (bf16[1024,2,128]{0,2,1:T(8,128)(2,1)S(1)}, bf16[1024,2,128]{0,2,1:T(8,128)(2,1)}, u32[]{:S(2)}) copy-start(bf16[1024,2,128]{0,2,1:T(8,128)(2,1)} %slice.273) | copy-start | bytes 1572868
  383.5 4.0 copy-start.12
  383.5 4.0 copy-start.19
  387.5 4.9 %copy-start.25 = (bf16[1024,2,128]{0,2,1:T(8,128)(2,1)S(1)}, bf16[1024,2,128]{0,2,1:T(8,128)(2,1)}, u32[]{:S(2)}) copy-start(bf16[1024,2,128]{0,2,1:T(8,128)(2,1)} %slice.283) | copy-start | bytes 1572868
  392.3 4.0 copy-start.11
  392.3 4.0 copy-start.18
  396.3 4.7 copy-start.24
  404.9 4.7 copy-start.23
  472.8 6.1 %copy-start.1 = (s32[8,16]{1,0:T(8,128)S(1)}, s32[8,16]{1,0:T(8,128)}, u32[]{:S(2)}) copy-start(s32[8,16]{1,0:T(8,128)} %param.7) | copy-start | bytes 1540
  (13 other events, 37.5 us)
where the time goes:
time: 486 us; the launch traced here: 479 us
  waiting for transfers between devices  234 us (48%)
  local copies, waits for them, and re-layouts  92.2 us (19%)
  matrix products  58.9 us (12%)
  blocking collectives  48.4 us (10%)
  starting transfers between devices  36.4 us (7%)
  other arithmetic  8.48 us (2%)
    ppermute x3, waiting for transfers between devices, shifted(): return lax.ppermute(block, axis, route)  206 us
    all_to_all x1, blocking collectives, attend(): lax.all_to_all(attended, 'seq', split_axis=0, concat_axis=2, tiled=True)  48.4 us
    sub x8, matrix products, attend(): exponent = jnp.exp(scores - row_max)  34.4 us
    slice x18, local copies, waits for them, and re-layouts, attend(): value_all[key_start:row_stop]  34.4 us
    all_to_all x1, waiting for transfers between devices, attend(): lax.all_to_all(query_split, 'seq', split_axis=1, concat_axis=0, tiled=True)  27.7 us
    dot_general x8, matrix products, attend(): jnp.einsum('hqk,khd->qhd', weights, value_all[key_start:row_stop], prefer...  24.5 us
    slice x17, local copies, waits for them, and re-layouts, attend(): query_block = query_all[row_start:row_stop]  15.1 us
    slice x18, local copies, waits for them, and re-layouts, attend(): key_all[key_start:row_stop]  14.2 us
  transfers between devices with their start and end apart: 6, of which 4 were waited for; matrix products, arithmetic and copies ran while one was open for 12% of the time, Pallas kernels for 0%

commit v1 on v0

v1 whole, which is shorter than its diff:
```python
import functools
import jax
import jax.numpy as jnp
from jax import lax
from jax.experimental import pallas as pl
from jax.experimental.pallas import tpu as pltpu
from jax.sharding import PartitionSpec as P

HEADS = 64
DQK = 192
DV = 128
DOCS = 16
LONGEST = 512
BLOCK = 128
CHUNKS = 2
GROUP = 16
NEGATIVE = -1e30


def attention_kernel(doc_starts, base, query, key_value, edge, out, window, sems):
    rows = query.shape[0]
    copies = (
        pltpu.make_async_copy(edge, window.at[pl.ds(0, LONGEST)], sems.at[0]),
        pltpu.make_async_copy(key_value, window.at[pl.ds(LONGEST, rows)], sems.at[1]),
    )
    for copy in copies:
        copy.start()
    for copy in copies:
        copy.wait()
    span = LONGEST + BLOCK
    first = base[0]
    lane = lax.broadcasted_iota(jnp.int32, (BLOCK, BLOCK), 1)
    sublane = lax.broadcasted_iota(jnp.int32, (BLOCK, BLOCK), 0)
    column = lax.broadcasted_iota(jnp.int32, (BLOCK, 256), 1)
    scale = DQK ** (-0.5)

    def block(number, carry):
        row = pl.multiple_of(number * BLOCK, BLOCK)
        position = first + row + sublane
        start = jnp.zeros((BLOCK, BLOCK), jnp.int32)
        for doc in range(1, DOCS):
            begin = doc_starts[doc]
            start = jnp.where(position >= begin, begin, start)
        start = start - (first + row - LONGEST)
        for head in range(2):
            queries = query[pl.ds(row, BLOCK), 128 * head : 128 * head + 256]
            inside = column < DQK if head == 0 else column >= 256 - DQK
            queries = jnp.where(inside, queries, jnp.zeros_like(queries))
            keys = window[pl.ds(row, span), 128 * head : 128 * head + 256]
            values = window[pl.ds(row, span), 384 + 128 * head : 512 + 128 * head]
            scores = lax.dot_general(
                queries, keys, (((1,), (1,)), ((), ())), preferred_element_type=jnp.float32
            )
            parts = []
            for part in range(span // BLOCK):
                piece = scores[:, part * BLOCK : (part + 1) * BLOCK]
                visible = lane + part * BLOCK >= start
                if part == span // BLOCK - 1:
                    visible = visible & (lane <= sublane)
                parts.append(jnp.where(visible, piece, NEGATIVE))
            scores = jnp.concatenate(parts, axis=1)
            top = jnp.max(scores, axis=1, keepdims=True)
            exponent = jnp.exp((scores - top) * scale)
            total = jnp.sum(exponent, axis=1, keepdims=True)
            weights = (exponent * (1.0 / total)).astype(jnp.bfloat16)
            mixed = jnp.dot(weights, values, preferred_element_type=jnp.float32)
            out[pl.ds(row, BLOCK), DV * head : DV * (head + 1)] = mixed.astype(jnp.bfloat16)
        return carry

    lax.fori_loop(0, rows // BLOCK, block, 0)


def attention(doc_starts, base, query, key_value, edge):
    rows = query.shape[0]
    return pl.pallas_call(
        attention_kernel,
        out_shape=jax.ShapeDtypeStruct((rows, 2 * DV), jnp.bfloat16),
        in_specs=[
            pl.BlockSpec(memory_space=pltpu.SMEM),
            pl.BlockSpec(memory_space=pltpu.SMEM),
            pl.BlockSpec(memory_space=pltpu.VMEM),
            pl.BlockSpec(memory_space=pl.ANY),
            pl.BlockSpec(memory_space=pl.ANY),
        ],
        out_specs=pl.BlockSpec(memory_space=pltpu.VMEM),
        scratch_shapes=[
            pltpu.VMEM((LONGEST + rows, 640), jnp.bfloat16),
            pltpu.SemaphoreType.DMA((2,)),
        ],
        name="attention",
    )(doc_starts, base, query, key_value, edge)


def exchange(block):
    groups = [[half * GROUP + i for i in range(GROUP)] for half in range(2)]
    return lax.all_to_all(
        block, "seq", split_axis=0, concat_axis=0, axis_index_groups=groups, tiled=True
    )


def local(queries, keys, values, doc_lengths):
    segment = lax.axis_index("pipe")
    half = lax.axis_index("seq") // GROUP
    lengths = lax.dynamic_index_in_dim(doc_lengths, segment, 0, keepdims=False)
    doc_starts = jnp.cumsum(lengths) - lengths
    rows = queries.shape[1]
    base = (half * GROUP * rows).astype(jnp.int32).reshape(1)
    heads = HEADS // CHUNKS // GROUP

    def chunk(array, number, width):
        columns = HEADS // CHUNKS * width
        piece = array[0, :, number * columns : (number + 1) * columns]
        return piece.reshape(rows, GROUP, heads * width).transpose(1, 0, 2)

    results = []
    for number in range(CHUNKS):
        key_value = jnp.concatenate(
            [chunk(keys, number, DQK), chunk(values, number, DV)], axis=2
        )
        key_value = exchange(key_value).reshape(GROUP * rows, heads * (DQK + DV))
        query = exchange(chunk(queries, number, DQK)).reshape(GROUP * rows, heads * DQK)
        edge = lax.ppermute(
            key_value[-LONGEST:], "seq", [(i, i + GROUP) for i in range(GROUP)]
        )
        attended = attention(doc_starts, base, query, key_value, edge)
        attended = exchange(attended.reshape(GROUP, rows, heads * DV))
        shifted = lax.ppermute(attended, "pipe", [(i, (i + 1) % 8) for i in range(8)])
        results.append(shifted.transpose(1, 0, 2).reshape(1, rows, HEADS // CHUNKS * DV))
    return jnp.concatenate(results, axis=2)


def solution(mesh):
    placed = (P("pipe", "seq", None), P("pipe", "seq", None), P("pipe", "seq", None), P())
    return jax.shard_map(
        local, mesh=mesh, in_specs=placed, out_specs=P("pipe", "seq", None), check_vma=False
    )
```

time: 486 us -> 262 us (0.54); the launches traced: 479 us -> 260 us
  waiting for transfers between devices: 234 us -> 136 us
  local copies, waits for them, and re-layouts: 92.2 us -> 25.8 us
  matrix products: 58.9 us -> 0 us
  blocking collectives: 48.4 us -> 0 us
  Pallas kernels: 0 us -> 42.3 us
  starting transfers between devices: 36.4 us -> 49.4 us
    ppermute x3 -> x4, waiting for transfers between devices: 206 us -> 50.4 us  [the longest x2 37.2 us: local(): lax.ppermute(key_value[-LONGEST:], 'seq', [(i, i + GROUP) for i in range(...]
    all_to_all x3 -> x6, waiting for transfers between devices: 27.7 us -> 85.7 us  [exchange(): lax.all_to_all(block, 'seq', split_axis=0, concat_axis=0, axis_index_grou...]
    slice x55 -> x5, local copies, waits for them, and re-layouts: 63.8 us -> 7.87 us  [the longest x3 6.66 us: chunk(): piece = array[0, :, number * columns:(number + 1) * columns]]
    all_to_all x1 -> x0, blocking collectives: 48.4 us -> none  [attend(): lax.all_to_all(attended, 'seq', split_axis=0, concat_axis=2, tiled=True)]
    pallas_call x0 -> x2, Pallas kernels: none -> 42.3 us  [attention(): pl.pallas_call(attention_kernel, out_shape=jax.ShapeDtypeStruct((rows, 2...]
    sub x8 -> x0, matrix products: 34.4 us -> none  [attend(): exponent = jnp.exp(scores - row_max)]
    dot_general x8 -> x0, matrix products: 24.5 us -> none  [attend(): jnp.einsum('hqk,khd->qhd', weights, value_all[key_start:row_stop], prefer...]
    ppermute x3 -> x4, starting transfers between devices: 0.17 us -> 16.7 us  [the longest x2 16.6 us: local(): lax.ppermute(key_value[-LONGEST:], 'seq', [(i, i + GROUP) for i in range(...]
  transfers between devices with their start and end apart: 6 -> 10, of which waited for: 4 -> 7; matrix products, arithmetic and copies ran while one was open for 12% -> 7% of each run, Pallas kernels for 0% -> 16%
where the time goes in v1:
time: 262 us; the launch traced here: 260 us
  waiting for transfers between devices  136 us (52%)
  starting transfers between devices  49.4 us (19%)
  Pallas kernels  42.3 us (16%)
  local copies, waits for them, and re-layouts  25.8 us (10%)
  other arithmetic  6.57 us (3%)
    all_to_all x6, waiting for transfers between devices, exchange(): lax.all_to_all(block, 'seq', split_axis=0, concat_axis=0, axis_index_grou...  85.7 us
    pallas_call x2, Pallas kernels, attention(): pl.pallas_call(attention_kernel, out_shape=jax.ShapeDtypeStruct((rows, 2...  42.3 us
    ppermute x2, waiting for transfers between devices, local(): lax.ppermute(key_value[-LONGEST:], 'seq', [(i, i + GROUP) for i in range(...  37.2 us
    all_to_all x6, starting transfers between devices, exchange(): lax.all_to_all(block, 'seq', split_axis=0, concat_axis=0, axis_index_grou...  32.7 us
    ppermute x2, starting transfers between devices, local(): lax.ppermute(key_value[-LONGEST:], 'seq', [(i, i + GROUP) for i in range(...  16.6 us
    ppermute x2, waiting for transfers between devices, local(): lax.ppermute(attended, 'pipe', [(i, (i + 1) % 8) for i in range(8)])  13.2 us
    unnamed x20, local copies, waits for them, and re-layouts  9.26 us
    slice x3, local copies, waits for them, and re-layouts, chunk(): piece = array[0, :, number * columns:(number + 1) * columns]  6.66 us
  transfers between devices with their start and end apart: 10, of which 7 were waited for; matrix products, arithmetic and copies ran while one was open for 7% of the time, Pallas kernels for 16%

profile of v1, /device:TPU:32, one launch (start us, length us, event | category | flops | bytes accessed | tf_op | source)
XLA Modules:
  0.0 260.4 jit_solution(12215244645387862592)
XLA Ops:
  0.0 2.1 fusion.2
  2.5 1.5 copy.38
  4.0 7.0 %all-to-all-start = ((bf16[16,128,384]{2,1,0:T(8,128)(2,1)}), bf16[16,128,384]{2,1,0:T(8,128)(2,1)S(1)}, u32[]{:S(2)}, u32[]{:S(2)}) async-start(bf16[16,128,384]{2,1,0:T(8,128)(2,1)} %bitcast.48), calls=%async_computation | async-start | bytes 3145728 | tf_op jit(solution)/shard_map/all_to_all | solution.py:96
  12.9 22.7 %all-to-all-done = bf16[16,128,384]{2,1,0:T(8,128)(2,1)S(1)} async-done(((bf16[16,128,384]{2,1,0:T(8,128)(2,1)}), bf16[16,128,384]{2,1,0:T(8,128)(2,1)S(1)}, u32[]{:S(2)}, u32[]{:S(2)}) %all-to-all-start) | async-done | bytes 1572896 | tf_op jit(solution)/shard_map/all_to_all | solution.py:96
  36.8 3.7 %all-to-all-start.3 = ((bf16[16,128,384]{2,1,0:T(8,128)(2,1)}), bf16[16,128,384]{2,1,0:T(8,128)(2,1)S(1)}, u32[]{:S(2)}, u32[]{:S(2)}) async-start(bf16[16,128,384]{2,1,0:T(8,128)(2,1)} %bitcast.46), calls=%async_computation.3 | async-start | bytes 3145728 | tf_op jit(solution)/shard_map/all_to_all | solution.py:96
  40.5 3.4 %fusion.1 = (bf16[1,128,6144]{2,1,0:T(8,128)(2,1)S(1)}, bf16[1,128,6144]{2,1,0:T(8,128)(2,1)}) fusion(bf16[1,128,12288]{2,1,0:T(8,128)(2,1)} %param.5), kind=kLoop, calls=%fused_computation.12 | loop fusion | bytes 6291456 | tf_op jit(solution)/shard_map/slice | solution.py:112
  47.6 1.8 pad_maximum_fusion
  49.4 14.4 %all-to-all-done.3 = bf16[16,128,384]{2,1,0:T(8,128)(2,1)S(1)} async-done(((bf16[16,128,384]{2,1,0:T(8,128)(2,1)}), bf16[16,128,384]{2,1,0:T(8,128)(2,1)S(1)}, u32[]{:S(2)}, u32[]{:S(2)}) %all-to-all-start.3) | async-done | bytes 1572896 | tf_op jit(solution)/shard_map/all_to_all | solution.py:96
  64.9 3.7 %all-to-all-start.1 = ((bf16[16,128,640]{2,1,0:T(8,128)(2,1)}), bf16[16,128,640]{2,1,0:T(8,128)(2,1)S(1)}, u32[]{:S(2)}, u32[]{:S(2)}) async-start(bf16[16,128,640]{2,1,0:T(8,128)(2,1)} %pad_maximum_fusion), calls=%async_computation.1 | async-start | bytes 5242880 | tf_op jit(solution)/shard_map/all_to_all | solution.py:96
  68.7 1.7 copy.27
  72.2 1.9 pad_maximum_fusion.1
  74.1 33.2 %all-to-all-done.1 = bf16[16,128,640]{2,1,0:T(8,128)(2,1)S(1)} async-done(((bf16[16,128,640]{2,1,0:T(8,128)(2,1)}), bf16[16,128,640]{2,1,0:T(8,128)(2,1)S(1)}, u32[]{:S(2)}, u32[]{:S(2)}) %all-to-all-start.1) | async-done | bytes 2621472 | tf_op jit(solution)/shard_map/all_to_all | solution.py:96
  107.3 4.5 %all-to-all-start.4 = ((bf16[16,128,640]{2,1,0:T(8,128)(2,1)}), bf16[16,128,640]{2,1,0:T(8,128)(2,1)}, u32[]{:S(2)}, u32[]{:S(2)}) async-start(bf16[16,128,640]{2,1,0:T(8,128)(2,1)} %pad_maximum_fusion.1), calls=%async_computation.4 | async-start | bytes 5242880 | tf_op jit(solution)/shard_map/all_to_all | solution.py:96
  111.8 8.2 %collective-permute-start = (bf16[512,640]{1,0:T(8,128)(2,1)S(1)}, bf16[512,640]{1,0:T(8,128)(2,1)S(1)}, u32[]{:S(2)}, u32[]{:S(2)}) collective-permute-start(bf16[512,640]{1,0:T(8,128)(2,1)S(1)} %bitcast.73), channel_id=1, source_target_pairs={{0,16},{1,17},{2,18},{3,19},{4,20},{5,21},{6,22},{7,23},{8,24},{9,... | collective-permute-start | bytes 1966088 | tf_op jit(solution)/shard_map/ppermute | solution.py:122
  122.3 24.3 %collective-permute-done.edge = bf16[512,640]{1,0:T(8,128)(2,1)S(1)} collective-permute-done((bf16[512,640]{1,0:T(8,128)(2,1)S(1)}, bf16[512,640]{1,0:T(8,128)(2,1)S(1)}, u32[]{:S(2)}, u32[]{:S(2)}) %collective-permute-start) | collective-permute-done | bytes 655392 | tf_op jit(solution)/shard_map/ppermute | solution.py:122
  147.4 21.2 %attention.2 = bf16[2048,256]{1,0:T(8,128)(2,1)} custom-call(s32[16]{0:T(128)} %bitcast_subtract_fusion.doc_starts, s32[1]{0:T(128)} %bitcast.2.base, bf16[2048,384]{1,0:T(8,128)(2,1)} %bitcast.57, bf16[2048,640]{1,0:T(8,128)(2,1)} %bitcast.51, bf16[512,640]{1,0:T(8,128)(2,1)} %copy-done.5), custom_call_target="tpu_custom_call" | custom-call | tf_op jit(solution)/shard_map/attention/pallas_call | solution.py:75
  168.6 6.8 %all-to-all-start.2 = ((bf16[16,128,256]{2,1,0:T(8,128)(2,1)}), bf16[16,128,256]{2,1,0:T(8,128)(2,1)S(1)}, u32[]{:S(2)}, u32[]{:S(2)}) async-start(bf16[16,128,256]{2,1,0:T(8,128)(2,1)} %bitcast.64), calls=%async_computation.2 | async-start | bytes 2097152 | tf_op jit(solution)/shard_map/all_to_all | solution.py:96
  176.6 8.3 %collective-permute-start.2 = (bf16[512,640]{1,0:T(8,128)(2,1)S(1)}, bf16[512,640]{1,0:T(8,128)(2,1)S(1)}, u32[]{:S(2)}, u32[]{:S(2)}) collective-permute-start(bf16[512,640]{1,0:T(8,128)(2,1)S(1)} %bitcast.74), channel_id=1, source_target_pairs={{0,16},{1,17},{2,18},{3,19},{4,20},{5,21},{6,22},{7,23},{8,24},{9,... | collective-permute-start | bytes 1966088 | tf_op jit(solution)/shard_map/ppermute | solution.py:122
  184.9 12.9 %collective-permute-done.2.edge = bf16[512,640]{1,0:T(8,128)(2,1)S(1)} collective-permute-done((bf16[512,640]{1,0:T(8,128)(2,1)S(1)}, bf16[512,640]{1,0:T(8,128)(2,1)S(1)}, u32[]{:S(2)}, u32[]{:S(2)}) %collective-permute-start.2) | collective-permute-done | bytes 655392 | tf_op jit(solution)/shard_map/ppermute | solution.py:122
  198.7 21.1 %attention.3 = bf16[2048,256]{1,0:T(8,128)(2,1)} custom-call(s32[16]{0:T(128)} %bitcast_subtract_fusion.doc_starts, s32[1]{0:T(128)} %bitcast.2.base, bf16[2048,384]{1,0:T(8,128)(2,1)} %bitcast.56, bf16[2048,640]{1,0:T(8,128)(2,1)} %bitcast.15.key_value, bf16[512,640]{1,0:T(8,128)(2,1)} %copy-done.6), custom_call_target="tpu_custom_call" | custom-call | tf_op jit(solution)/shard_map/attention/pallas_call | solution.py:75
  219.9 6.9 %all-to-all-start.5 = ((bf16[16,128,256]{2,1,0:T(8,128)(2,1)}), bf16[16,128,256]{2,1,0:T(8,128)(2,1)S(1)}, u32[]{:S(2)}, u32[]{:S(2)}) async-start(bf16[16,128,256]{2,1,0:T(8,128)(2,1)} %bitcast.65), calls=%async_computation.5 | async-start | bytes 2097152 | tf_op jit(solution)/shard_map/all_to_all | solution.py:96
  226.9 15.4 %all-to-all-done.5 = bf16[16,128,256]{2,1,0:T(8,128)(2,1)S(1)} async-done(((bf16[16,128,256]{2,1,0:T(8,128)(2,1)}), bf16[16,128,256]{2,1,0:T(8,128)(2,1)S(1)}, u32[]{:S(2)}, u32[]{:S(2)}) %all-to-all-start.5) | async-done | bytes 1048608 | tf_op jit(solution)/shard_map/all_to_all | solution.py:96
  243.4 13.2 %collective-permute-done.3 = bf16[16,128,256]{2,1,0:T(8,128)(2,1)} collective-permute-done((bf16[16,128,256]{2,1,0:T(8,128)(2,1)S(1)}, bf16[16,128,256]{2,1,0:T(8,128)(2,1)}, u32[]{:S(2)}, u32[]{:S(2)}) %collective-permute-start.3) | collective-permute-done | bytes 1048608 | tf_op jit(solution)/shard_map/ppermute | solution.py:127
  256.6 1.8 copy.22
  (41 shorter events, 18.2 us)
Async XLA Ops:
  4.0 31.6 %all-to-all-start = ((bf16[16,128,384]{2,1,0:T(8,128)(2,1)}), bf16[16,128,384]{2,1,0:T(8,128)(2,1)S(1)}, u32[]{:S(2)}, u32[]{:S(2)}) async-start(bf16[16,128,384]{2,1,0:T(8,128)(2,1)} %bitcast.48), calls=%async_computation | async-start | bytes 3145728 | tf_op jit(solution)/shard_map/all_to_all | solution.py:96
  35.6 1.3 copy-start.2
  36.8 27.0 %all-to-all-start.3 = ((bf16[16,128,384]{2,1,0:T(8,128)(2,1)}), bf16[16,128,384]{2,1,0:T(8,128)(2,1)S(1)}, u32[]{:S(2)}, u32[]{:S(2)}) async-start(bf16[16,128,384]{2,1,0:T(8,128)(2,1)} %bitcast.46), calls=%async_computation.3 | async-start | bytes 3145728 | tf_op jit(solution)/shard_map/all_to_all | solution.py:96
  44.2 1.6 copy-start.4
  63.8 1.1 copy-start.1
  64.9 42.3 %all-to-all-start.1 = ((bf16[16,128,640]{2,1,0:T(8,128)(2,1)}), bf16[16,128,640]{2,1,0:T(8,128)(2,1)S(1)}, u32[]{:S(2)}, u32[]{:S(2)}) async-start(bf16[16,128,640]{2,1,0:T(8,128)(2,1)} %pad_maximum_fusion), calls=%async_computation.1 | async-start | bytes 5242880 | tf_op jit(solution)/shard_map/all_to_all | solution.py:96
  70.4 1.2 copy-start.3
  107.3 4.5 %copy-start = (bf16[16,128,640]{2,1,0:T(8,128)(2,1)}, bf16[16,128,640]{2,1,0:T(8,128)(2,1)S(1)}, u32[]{:S(2)}) copy-start(bf16[16,128,640]{2,1,0:T(8,128)(2,1)S(1)} %all-to-all-done.1) | copy-start | bytes 7864324
  107.3 61.3 %all-to-all-start.4 = ((bf16[16,128,640]{2,1,0:T(8,128)(2,1)}), bf16[16,128,640]{2,1,0:T(8,128)(2,1)}, u32[]{:S(2)}, u32[]{:S(2)}) async-start(bf16[16,128,640]{2,1,0:T(8,128)(2,1)} %pad_maximum_fusion.1), calls=%async_computation.4 | async-start | bytes 5242880 | tf_op jit(solution)/shard_map/all_to_all | solution.py:96
  111.8 34.8 %collective-permute-start = (bf16[512,640]{1,0:T(8,128)(2,1)S(1)}, bf16[512,640]{1,0:T(8,128)(2,1)S(1)}, u32[]{:S(2)}, u32[]{:S(2)}) collective-permute-start(bf16[512,640]{1,0:T(8,128)(2,1)S(1)} %bitcast.73), channel_id=1, source_target_pairs={{0,16},{1,17},{2,18},{3,19},{4,20},{5,21},{6,22},{7,23},{8,24},{9,... | collective-permute-start | bytes 1966088 | tf_op jit(solution)/shard_map/ppermute | solution.py:122
  146.6 0.8 copy-start.5
  168.6 51.2 %all-to-all-start.2 = ((bf16[16,128,256]{2,1,0:T(8,128)(2,1)}), bf16[16,128,256]{2,1,0:T(8,128)(2,1)S(1)}, u32[]{:S(2)}, u32[]{:S(2)}) async-start(bf16[16,128,256]{2,1,0:T(8,128)(2,1)} %bitcast.64), calls=%async_computation.2 | async-start | bytes 2097152 | tf_op jit(solution)/shard_map/all_to_all | solution.py:96
  176.6 21.3 %collective-permute-start.2 = (bf16[512,640]{1,0:T(8,128)(2,1)S(1)}, bf16[512,640]{1,0:T(8,128)(2,1)S(1)}, u32[]{:S(2)}, u32[]{:S(2)}) collective-permute-start(bf16[512,640]{1,0:T(8,128)(2,1)S(1)} %bitcast.74), channel_id=1, source_target_pairs={{0,16},{1,17},{2,18},{3,19},{4,20},{5,21},{6,22},{7,23},{8,24},{9,... | collective-permute-start | bytes 1966088 | tf_op jit(solution)/shard_map/ppermute | solution.py:122
  197.9 0.8 copy-start.6
  219.9 22.4 %all-to-all-start.5 = ((bf16[16,128,256]{2,1,0:T(8,128)(2,1)}), bf16[16,128,256]{2,1,0:T(8,128)(2,1)S(1)}, u32[]{:S(2)}, u32[]{:S(2)}) async-start(bf16[16,128,256]{2,1,0:T(8,128)(2,1)} %bitcast.65), calls=%async_computation.5 | async-start | bytes 2097152 | tf_op jit(solution)/shard_map/all_to_all | solution.py:96
  226.8 15.4 %collective-permute-start.1 = (bf16[16,128,256]{2,1,0:T(8,128)(2,1)S(1)}, bf16[16,128,256]{2,1,0:T(8,128)(2,1)S(1)}, u32[]{:S(2)}, u32[]{:S(2)}) collective-permute-start(bf16[16,128,256]{2,1,0:T(8,128)(2,1)S(1)} %all-to-all-done.2), channel_id=1, source_target_pairs={{0,32},{32,64},{64,96},{96,128},{128,160},{160,192},{192,224},{224... | collective-permute-start | bytes 3145736 | tf_op jit(solution)/shard_map/ppermute | solution.py:127
  242.3 14.3 %collective-permute-start.3 = (bf16[16,128,256]{2,1,0:T(8,128)(2,1)S(1)}, bf16[16,128,256]{2,1,0:T(8,128)(2,1)}, u32[]{:S(2)}, u32[]{:S(2)}) collective-permute-start(bf16[16,128,256]{2,1,0:T(8,128)(2,1)S(1)} %all-to-all-done.5), channel_id=1, source_target_pairs={{0,32},{32,64},{64,96},{96,128},{128,160},{160,192},{192,224},{224... | collective-permute-start | bytes 3145736 | tf_op jit(solution)/shard_map/ppermute | solution.py:127
